TPU v7x, 256 devices: a whole 4x4x8 slice. The times are simulated.
256 devices in a mesh: ctx: 8 (over z), chan: 32 (over x, y, core).
Axes of the slice: x: 4, y: 4, z: 8, core: 2. Of those that a mesh axis runs over, the one named last changes fastest.
Arguments:
- query_rows: bfloat16 [2048, 8192], P('ctx', 'chan'), may hold values from -6 to 6
- key_rows: bfloat16 [2048, 8192], P('ctx', 'chan'), may hold values from -6 to 6
- value_rows: bfloat16 [2048, 8192], P('ctx', 'chan'), may hold values from -6 to 6
- short_taps: float32 [3, 3, 8192], P(None, None, 'chan'), may hold values from -3 to 3
- long_filter: bfloat16 [2048, 8192], P('ctx', 'chan'), may hold values from -4 to 4
- direction: bfloat16 [2048, 8192], P('ctx', 'chan'), may hold values from -4 to 4
- w_out: bfloat16 [8192, 8192], P('chan'), may hold values from -0.125 to 0.125
- target: bfloat16 [2048, 8192], P('ctx'), may hold values from -6 to 6
Outputs:
- grad_filter: float32 [2048, 8192], P('ctx', 'chan')
- hvp_filter: float32 [2048, 8192], P('ctx', 'chan')
All inputs are finite; a program needn't handle non-finite values.
Results may differ from a plain program's by a relative error of at most 0.033.
Values may be sent and summed in bfloat16 or wider, within the bound.
A program may use at most 128 MiB of HBM per device.

v0:
```python
import math

import jax
import jax.numpy as jnp
from jax import lax
from jax.sharding import PartitionSpec as P


def passed_along(value, axis, steps):
    count = lax.axis_size(axis)
    initial, last = (max(0, -steps), min(count, count - steps))
    return lax.ppermute(value, axis, [(source, source + steps) for source in range(initial, last)])


def short_conv(current, earlier, coeffs):
    extended = jnp.concatenate([earlier.astype(jnp.float32), current.astype(jnp.float32)], axis=0)
    length = current.shape[0]
    return (
        coeffs[0] * extended[2 : 2 + length]
        + coeffs[1] * extended[1 : 1 + length]
        + coeffs[2] * extended[0:length]
    )


def depthwise(window, kernel):
    result = lax.conv_general_dilated(
        window[None],
        kernel[:, None, :],
        (1,),
        "VALID",
        dimension_numbers=("NHC", "HIO", "NHC"),
        feature_group_count=window.shape[1],
        preferred_element_type=jnp.float32,
    )
    return result[0]


def paired(window, first_kernel, second_kernel):
    return jax.vmap(lambda kernel: depthwise(window, kernel))(
        jnp.stack([first_kernel, second_kernel])
    )


def on_device(query_rows, key_rows, value_rows, short_taps, long_filter, direction, w_out, target):
    block_len = query_rows.shape[0]
    chan_width = query_rows.shape[1]
    earlier = passed_along(
        (query_rows[block_len - 2 :], key_rows[block_len - 2 :], value_rows[block_len - 2 :]),
        "ctx",
        1,
    )
    taps_all, dir_all = (
        lax.all_gather(long_filter, "ctx", axis=0, tiled=True),
        lax.all_gather(direction, "ctx", axis=0, tiled=True),
    )
    gate_in = short_conv(query_rows, earlier[0], short_taps[0])
    key_short = short_conv(key_rows, earlier[1], short_taps[1])
    value_short = short_conv(value_rows, earlier[2], short_taps[2])
    mixed_rows = (key_short * value_short).astype(jnp.bfloat16)
    history = lax.all_gather(mixed_rows, "ctx", axis=0, tiled=True)
    seq_total = history.shape[0]
    my_block = lax.axis_index("ctx")
    padded = jnp.concatenate([jnp.zeros((block_len, chan_width), jnp.bfloat16), history], axis=0)

    def window_at(distance):
        return lax.dynamic_slice_in_dim(padded, distance * block_len + 1, 2 * block_len - 1, 0)

    def forward_step(tap_block, running):
        window = window_at(my_block - tap_block)
        taps_here = lax.dynamic_slice_in_dim(taps_all, tap_block * block_len, block_len, 0)[::-1]
        dirs_here = lax.dynamic_slice_in_dim(dir_all, tap_block * block_len, block_len, 0)[::-1]
        return running + paired(window, taps_here, dirs_here)

    convolved = lax.fori_loop(
        0, my_block + 1, forward_step, jnp.zeros((2, block_len, chan_width), jnp.float32)
    )
    gated_rows = (gate_in * convolved[0]).astype(jnp.bfloat16)
    gated_dir = (gate_in * convolved[1]).astype(jnp.bfloat16)
    stacked = jnp.concatenate([gated_rows, gated_dir], axis=0)
    scaling = 1.0 / math.sqrt(seq_total)
    summed = lax.psum_scatter(
        lax.dot_general(
            w_out, stacked, (((0,), (1,)), ((), ())), preferred_element_type=jnp.float32
        ).astype(jnp.bfloat16),
        "chan",
        scatter_dimension=0,
        tiled=True,
    ).astype(jnp.float32)
    column_start = lax.axis_index("chan") * chan_width
    target_mine = (
        lax.dynamic_slice_in_dim(target, column_start, chan_width, 1).astype(jnp.float32).T
    )
    bent_out = jnp.tanh(summed[:, :block_len] - target_mine)
    cot_grad = (scaling * bent_out).astype(jnp.bfloat16)
    cot_hvp = (scaling * (1.0 - bent_out * bent_out) * summed[:, block_len:]).astype(jnp.bfloat16)
    cotangent = jnp.concatenate([cot_grad, cot_hvp], axis=1)
    backward = jnp.dot(
        w_out,
        lax.all_gather(cotangent, "chan", axis=0, tiled=True),
        preferred_element_type=jnp.float32,
    )
    back_grad = backward[:, :block_len].T
    back_hvp = backward[:, block_len:].T
    dz_grad = (gate_in * back_grad).astype(jnp.bfloat16)
    dz_hvp = (gate_in * back_hvp).astype(jnp.bfloat16)

    def backward_step(tap_block, running):
        window = window_at(my_block - tap_block)
        pair = paired(window, dz_grad, dz_hvp)[:, ::-1]
        placed = jnp.concatenate([pair[0], pair[1]], axis=1)
        return lax.dynamic_update_slice_in_dim(running, placed, tap_block * block_len, 0)

    tap_terms = lax.fori_loop(
        0, my_block + 1, backward_step, jnp.zeros((seq_total, 2 * chan_width), jnp.float32)
    )
    shares = lax.psum_scatter(
        tap_terms.astype(jnp.bfloat16), "ctx", scatter_dimension=0, tiled=True
    ).astype(jnp.float32)
    return (shares[:, :chan_width], shares[:, chan_width:])


def solution(mesh):
    in_specs = (
        P("ctx", "chan"),
        P("ctx", "chan"),
        P("ctx", "chan"),
        P(None, None, "chan"),
        P("ctx", "chan"),
        P("ctx", "chan"),
        P("chan", None),
        P("ctx", None),
    )
    out_specs = (P("ctx", "chan"), P("ctx", "chan"))
    return jax.shard_map(
        on_device, mesh=mesh, in_specs=in_specs, out_specs=out_specs, check_vma=False
    )
```

profile of v0, /device:TPU:1, one launch (start us, length us, event | category | flops | bytes accessed | tf_op | source)
XLA Modules:
  0.0 612.1 jit_solution(8180843435490185184)
XLA Ops:
  7.2 0.0 all-gather.5.cloned.1.call-start
  7.2 0.7 slice.125
  7.9 4.3 collective-permute-start
  12.3 0.7 slice.131
  13.0 3.5 collective-permute-start.1
  16.5 1.5 fusion.41
  17.9 0.9 convert_element_type.55
  18.9 0.9 convert_element_type.57
  19.8 0.0 collective-permute-done
  19.8 0.0 collective-permute-done.1
  19.8 0.8 fusion.14
  20.7 0.0 all-gather.5.cloned.1.call-update
  20.7 0.0 all-gather.7.cloned.1.call-start
  20.8 0.7 all-gather.7.cloned.1.call-update
  21.5 0.0 all-gather.9.cloned.1.call-start
  21.5 0.7 all-gather.9.cloned.1.call-update
  22.2 0.0 reduce-scatter.3.cloned.1.call-start
  22.2 0.7 slice.137
  22.9 3.5 collective-permute-start.2
  26.5 1.6 convert_element_type.60
  28.1 0.0 collective-permute-done.2
  28.1 0.6 convert_element_type.61
  28.7 27.7 %all-gather.5.cloned.1.call-done = bf16[2048,256]{1,0:T(8,128)(2,1)} async-done(((bf16[256,256]{1,0:T(8,128)(2,1)}), bf16[2048,256]{1,0:T(8,128)(2,1)}) %all-gather.5.cloned.1.call-update) | async-done | bytes 1048592 | tf_op jit(solution)/shard_map/all_gather | solution.py:60
  56.4 1.3 concatenate.26
  57.7 37.3 %all-gather.7.cloned.1.call-done = bf16[2048,256]{1,0:T(8,128)(2,1)} async-done(((bf16[256,256]{1,0:T(8,128)(2,1)}), bf16[2048,256]{1,0:T(8,128)(2,1)}) %all-gather.7.cloned.1.call-update) | async-done | bytes 1048592 | tf_op jit(solution)/shard_map/all_gather | solution.py:53
  95.0 38.6 %all-gather.9.cloned.1.call-done = bf16[2048,256]{1,0:T(8,128)(2,1)} async-done(((bf16[256,256]{1,0:T(8,128)(2,1)}), bf16[2048,256]{1,0:T(8,128)(2,1)}) %all-gather.9.cloned.1.call-update) | async-done | bytes 1048592 | tf_op jit(solution)/shard_map/all_gather | solution.py:54
  133.6 0.1 broadcast_in_dim.22
  133.8 0.0 copy-start
  133.8 0.0 copy-start.1
  133.8 0.0 copy-start.2
  133.8 0.0 copy-start.3
  133.8 0.0 copy-start.4
  133.8 15.6 %while.24 = (s32[]{:T(128)}, f32[2,256,256]{2,0,1:T(2,128)S(1)}, s32[]{:T(128)}, s32[]{:T(128)}, bf16[2304,256]{1,0:T(8,128)(2,1)S(1)}, /*index=5*/bf16[2048,256...) while((s32[]{:T(128)}, f32[2,256,256]{2,0,1:T(2,128)S(1)}, ...), condition=%wide.region_1.0_spmd, body=%wide.region_0.0_spmd.sunk | while | flops 67371016 | bytes 4717297 | solution.py:74
  133.8 1.0 constant_dynamic-slice_fusion.3
  134.9 0.2 rev.15
  135.1 0.2 rev.16
  135.3 0.1 dynamic-slice_bitcast_fusion.4
  135.4 13.5 %convolution_bitcast_fusion.5 = f32[2,1,256,256]{3,1,0,2:T(1,128)S(1)} fusion(bf16[256,1,256,2]{2,0,3,1:T(8,128)(2,1)S(1)} %maximum_bitcast_fusion.2, bf16[1,511,256,1]{2,1,3,0:T(8,128)(2,1)S(1)} %dynamic-slice_bitcast_fusion.4), kind=kOutput, calls=%fused_computation.clone.1 | convolution fusion | flops 67108864 | bytes 1048064 | tf_op jit(solution)/shard_map/convolution.6
  148.9 0.6 bitcast_add_fusion.2
  149.5 0.1 fusion.28
  149.7 7.8 %fusion.4 = bf16[8192,512]{0,1:T(8,128)(2,1)} fusion(bf16[256,8192]{1,0:T(8,128)(2,1)} %param.18, bf16[256,256]{1,0:T(8,128)(2,1)S(1)} %fusion.26, bf16[256,256]{1,0:T(8,128)(2,1)S(1)} %get-tuple-element.225), kind=kOutput, calls=%fused_computation.17 | convolution fusion | flops 2152202240 | bytes 12845056 | tf_op jit(solution)/shard_map/dot_general | solution.py:82
  157.5 0.0 reduce-scatter.3.cloned.1.call-update
  157.5 0.0 all-gather.11.cloned.1.call-start
  157.6 209.8 %reduce-scatter.3.cloned.1.call-done = bf16[256,512]{0,1:T(8,128)(2,1)} async-done(((bf16[8192,512]{0,1:T(8,128)(2,1)}), bf16[256,512]{0,1:T(8,128)(2,1)}) %reduce-scatter.3.cloned.1.call-update) | async-done | bytes 262160 | tf_op jit(solution)/shard_map/reduce_scatter | solution.py:81
  367.4 1.0 convert_element_type.66
  368.4 1.0 multiply_convert_fusion
  369.4 0.7 pad_maximum_fusion.3
  370.1 0.0 all-gather.11.cloned.1.call-update
  370.2 0.2 reduce-scatter.5.cloned.1.call-start
  370.4 65.2 %all-gather.11.cloned.1.call-done = bf16[8192,512]{0,1:T(8,128)(2,1)} async-done(((bf16[256,512]{0,1:T(8,128)(2,1)}), bf16[8192,512]{0,1:T(8,128)(2,1)}) %all-gather.11.cloned.1.call-update) | async-done | bytes 8388624 | tf_op jit(solution)/shard_map/all_gather | solution.py:99
  435.6 6.9 %convolution_bitcast_fusion.2 = f32[256,512]{0,1:T(8,128)S(1)} fusion(bf16[8192,512]{0,1:T(8,128)(2,1)} %all-gather.11.cloned.1.call-done, bf16[256,8192]{1,0:T(8,128)(2,1)} %param.18), kind=kOutput, calls=%fused_computation.18 | convolution fusion | flops 2147483648 | bytes 13107200 | tf_op jit(solution)/shard_map/dot_general | solution.py:97
  442.6 0.1 fusion.35
  442.7 0.3 copy.22
  442.9 1.5 broadcast_in_dim.21
  444.4 15.5 %while.25 = (s32[]{:T(128)}, bf16[2048,512]{1,0:T(8,128)(2,1)}, s32[]{:T(128)}, s32[]{:T(128)}, bf16[2304,256]{1,0:T(8,128)(2,1)S(1)}, /*index=5*/bf16[2,256,256...) while((s32[]{:T(128)}, bf16[2048,512]{1,0:T(8,128)(2,1)}, ...), condition=%wide.region_4.0_spmd, body=%wide.region_3.0_spmd.sunk | while | flops 67633160 | bytes 3406569 | solution.py:113
  444.4 0.1 dynamic-slice_bitcast_fusion.5
  444.5 13.6 %convolution_bitcast_fusion.6 = bf16[2,1,256,256]{3,1,0,2:T(2,128)(2,1)S(1)} fusion(bf16[256,1,256,2]{2,3,0,1:T(2,128)(2,1)S(1)} %bitcast.127, bf16[1,511,256,1]{2,1,3,0:T(8,128)(2,1)S(1)} %dynamic-slice_bitcast_fusion.5), kind=kOutput, calls=%fused_computation.8.clone.1 | convolution fusion | flops 67108864 | bytes 785920 | tf_op jit(solution)/shard_map/convolution.7
  458.1 0.5 fusion.54
  458.6 0.3 slice.260
  459.0 0.2 slice.261
  459.2 0.7 maximum_dynamic-update-slice_fusion.2
  459.9 0.0 reduce-scatter.5.cloned.1.call-update
  459.9 143.5 %reduce-scatter.5.cloned.1.call-done = bf16[256,512]{1,0:T(8,128)(2,1)} async-done(((bf16[2048,512]{1,0:T(8,128)(2,1)}), bf16[256,512]{1,0:T(8,128)(2,1)}) %reduce-scatter.5.cloned.1.call-update) | async-done | bytes 262160 | tf_op jit(solution)/shard_map/reduce_scatter | solution.py:116
  603.4 1.8 fusion.40
  (13 shorter events, 0.2 us)
Async XLA Ops:
  7.2 49.2 %all-gather.5.cloned.1.call-start = ((), (), s32[]{:S(2)}) async-start(), calls=%async_computation.2 | async-start | bytes 1179648 | tf_op jit(solution)/shard_map/all_gather | solution.py:60
  7.9 11.9 %collective-permute-start = (bf16[2,256]{1,0:T(2,128)(2,1)S(1)}, bf16[2,256]{1,0:T(2,128)(2,1)S(1)}, u32[]{:S(2)}, u32[]{:S(2)}) collective-permute-start(bf16[2,256]{1,0:T(2,128)(2,1)S(1)} %slice.125), channel_id=1, source_target_pairs={{0,32},{32,64},{64,96},{96,128},{128,160},{160,192},{192,224},{1,3... | collective-permute-start | bytes 3080 | tf_op jit(solution)/shard_map/ppermute | solution.py:12
  13.0 6.9 %collective-permute-start.1 = (bf16[2,256]{1,0:T(2,128)(2,1)S(1)}, bf16[2,256]{1,0:T(2,128)(2,1)S(1)}, u32[]{:S(2)}, u32[]{:S(2)}) collective-permute-start(bf16[2,256]{1,0:T(2,128)(2,1)S(1)} %slice.131), channel_id=1, source_target_pairs={{0,32},{32,64},{64,96},{96,128},{128,160},{160,192},{192,224},{1,3... | collective-permute-start | bytes 3080 | tf_op jit(solution)/shard_map/ppermute | solution.py:12
  20.7 74.3 %all-gather.7.cloned.1.call-start = ((), (), s32[]{:S(2)}) async-start(), calls=%async_computation.3 | async-start | bytes 1179648 | tf_op jit(solution)/shard_map/all_gather | solution.py:53
  21.5 112.2 %all-gather.9.cloned.1.call-start = ((), (), s32[]{:S(2)}) async-start(), calls=%async_computation.4 | async-start | bytes 1179648 | tf_op jit(solution)/shard_map/all_gather | solution.py:54
  22.2 345.2 %reduce-scatter.3.cloned.1.call-start = ((), (), s32[]{:S(2)}) async-start(), calls=%async_computation.5 | async-start | bytes 8650752 | tf_op jit(solution)/shard_map/reduce_scatter | solution.py:81
  22.9 5.2 collective-permute-start.2
  133.8 15.7 %copy-start = (f32[256,256]{1,0:T(8,128)S(1)}, f32[256,256]{1,0:T(8,128)}, u32[]{:S(2)}) copy-start(f32[256,256]{1,0:T(8,128)} %convert_element_type.60) | copy-start | bytes 786436
  133.8 15.7 %copy-start.1 = (f32[2,256]{1,0:T(2,128)S(1)}, f32[2,256]{1,0:T(2,128)}, u32[]{:S(2)}) copy-start(f32[2,256]{1,0:T(2,128)} %convert_element_type.61) | copy-start | bytes 6148
  133.8 15.7 %copy-start.2 = (f32[1,1,256]{2,1,0:T(1,128)S(1)}, f32[1,1,256]{2,1,0:T(1,128)}, u32[]{:S(2)}) copy-start(f32[1,1,256]{2,1,0:T(1,128)} %get-tuple-element.237) | copy-start | bytes 3076
  133.8 15.7 %copy-start.3 = (f32[1,1,256]{2,1,0:T(1,128)S(1)}, f32[1,1,256]{2,1,0:T(1,128)}, u32[]{:S(2)}) copy-start(f32[1,1,256]{2,1,0:T(1,128)} %get-tuple-element.244) | copy-start | bytes 3076
  133.8 15.7 %copy-start.4 = (f32[1,1,256]{2,1,0:T(1,128)S(1)}, f32[1,1,256]{2,1,0:T(1,128)}, u32[]{:S(2)}) copy-start(f32[1,1,256]{2,1,0:T(1,128)} %get-tuple-element.245) | copy-start | bytes 3076
  157.5 278.1 %all-gather.11.cloned.1.call-start = ((), (), s32[]{:S(2)}) async-start(), calls=%async_computation.6 | async-start | bytes 8650752 | tf_op jit(solution)/shard_map/all_gather | solution.py:99
  370.2 233.3 %reduce-scatter.5.cloned.1.call-start = ((), (), s32[]{:S(2)}) async-start(), calls=%async_computation.7 | async-start | bytes 2359296 | tf_op jit(solution)/shard_map/reduce_scatter | solution.py:116
Sparse Core Ops, SparseCore 0:
  20.8 35.5 all-gather.4
  58.2 36.7 all-gather.6
  96.8 36.7 all-gather.8
  157.6 209.7 reduce-scatter.2
  370.3 65.2 all-gather.10
  460.0 143.3 reduce-scatter.4
where the time goes:
time: 616 us; the launch traced here: 612 us
  waiting for transfers between devices  524 us (85%)
  matrix products  41.8 us (7%)
  between operations  14.3 us (2%)
  starting transfers between devices  11.8 us (2%)
  local copies, waits for them, and re-layouts  11.1 us (2%)
  other arithmetic  9.17 us (1%)
    reduce_scatter x1, waiting for transfers between devices, on_device(): lax.psum_scatter(lax.dot_general(w_out, stacked, (((0,), (1,)), ((), ()))...  210 us
    reduce_scatter x1, waiting for transfers between devices, on_device(): lax.psum_scatter(tap_terms.astype(jnp.bfloat16), 'ctx', scatter_dimension...  144 us
    all_gather x1, waiting for transfers between devices, on_device(): lax.all_gather(cotangent, 'chan', axis=0, tiled=True)  65.2 us
    all_gather x1, waiting for transfers between devices, on_device(): lax.all_gather(direction, 'ctx', axis=0, tiled=True)  38.6 us
    all_gather x1, waiting for transfers between devices, on_device(): lax.all_gather(long_filter, 'ctx', axis=0, tiled=True)  37.3 us
    all_gather x1, waiting for transfers between devices, on_device(): history = lax.all_gather(mixed_rows, 'ctx', axis=0, tiled=True)  27.7 us
    another operation x2, matrix products  27.1 us
  transfers between devices with their start and end apart: 9, of which 6 were waited for; matrix products, arithmetic and copies ran while one was open for 1% of the time, Pallas kernels for 0%

commit v1 on v0

v1 whole, which is shorter than its diff:
```python
import functools
import math

import jax
import jax.numpy as jnp
from jax import lax
from jax.experimental import pallas as pl
from jax.experimental.pallas import tpu as pltpu
from jax.sharding import PartitionSpec as P

MESH = pl.DeviceIdType.MESH
BF = jnp.bfloat16
F32 = jnp.float32
VM = pl.BlockSpec(memory_space=pltpu.VMEM)
ANY = pl.BlockSpec(memory_space=pl.ANY)
NZ = 8
NR = 4
BL = 256
LN = 128
CW = BL // NZ


class Copies:
    def __init__(self, send_sems, recv_sems):
        self.send_sems, self.recv_sems, self.made = send_sems, recv_sems, []

    def start(self, src, dst, device):
        slot = len(self.made)
        copy = pltpu.make_async_remote_copy(
            src_ref=src,
            dst_ref=dst,
            send_sem=self.send_sems.at[slot],
            recv_sem=self.recv_sems.at[slot],
            device_id=device,
            device_id_type=MESH,
        )
        copy.start()
        self.made.append(copy)
        return copy

    def drain(self):
        for copy in self.made:
            copy.wait_send()


def barrier(devices):
    sem = pltpu.get_barrier_semaphore()
    for device in devices:
        pl.semaphore_signal(sem, inc=1, device_id=device, device_id_type=MESH)
    pl.semaphore_wait(sem, len(devices))


def z_peers(z):
    return [{"ctx": lax.rem(z + off, NZ)} for off in range(1, NZ)]


def enter_kernel(
    q_ref, k_ref, v_ref, taps_ref, h_ref, d_ref, w_ref,
    gate_ref, got_ref, wp_ref,
    halo, ext, out_buf, in_buf, send_sems, recv_sems,
):
    z, c = lax.axis_index("ctx"), lax.axis_index("chan")
    core = lax.rem(c, 2)
    partner = {"chan": c + 1 - 2 * core}
    barrier(z_peers(z) + [partner])
    cp = Copies(send_sems, recv_sems)
    half = w_ref.shape[1] // 2
    after = {"ctx": lax.rem(z + 1, NZ)}
    halos = [
        cp.start(ref.at[pl.ds(BL - 16, 16)], halo.at[i], after)
        for i, ref in enumerate((q_ref, k_ref, v_ref))
    ]
    w_copy = cp.start(
        w_ref.at[:, pl.ds(pl.multiple_of((1 - core) * half, LN), half)], wp_ref, partner
    )

    def put(value, which):
        for jj in range(2):
            turned = value[jj * LN : (jj + 1) * LN].T
            out_buf[:, which, jj] = turned.reshape(NZ, CW, LN).astype(BF)

    put(h_ref[...].astype(F32), 0)
    put(d_ref[...].astype(F32), 1)
    arrivals = []
    for off in range(1, NZ):
        to = lax.rem(z + off, NZ)
        arrivals.append(
            cp.start(out_buf.at[to, pl.ds(0, 2)], in_buf.at[z, pl.ds(0, 2)], {"ctx": to})
        )
    for copy in halos:
        copy.wait_recv()
    inside = (z > 0).astype(F32)
    short = []
    for i, ref in enumerate((q_ref, k_ref, v_ref)):
        ext[i, pl.ds(0, 16)] = halo[i].astype(F32) * inside
        ext[i, pl.ds(16, BL)] = ref[...].astype(F32)
        short.append(
            taps_ref[pl.ds(3 * i, 1)] * ext[i, pl.ds(16, BL)]
            + taps_ref[pl.ds(3 * i + 1, 1)] * ext[i, pl.ds(15, BL)]
            + taps_ref[pl.ds(3 * i + 2, 1)] * ext[i, pl.ds(14, BL)]
        )
    gate_ref[...] = short[0]
    put(short[1] * short[2], 2)
    for off in range(1, NZ):
        to = lax.rem(z + off, NZ)
        arrivals.append(cp.start(out_buf.at[to, 2], in_buf.at[z, 2], {"ctx": to}))
    in_buf[z] = out_buf[z]
    for copy in arrivals:
        copy.wait_recv()
    got_ref[...] = in_buf[...]
    w_copy.wait_recv()
    cp.drain()


def enter(q, k, v, taps, h, d, w):
    return pl.pallas_call(
        enter_kernel,
        out_shape=(
            jax.ShapeDtypeStruct((BL, BL), F32),
            jax.ShapeDtypeStruct((NZ, 3, 2, CW, LN), BF),
            jax.ShapeDtypeStruct((BL, w.shape[1] // 2), BF),
        ),
        in_specs=[VM] * 6 + [ANY],
        out_specs=(VM, VM, ANY),
        scratch_shapes=[
            pltpu.VMEM((3, 16, BL), BF),
            pltpu.VMEM((3, BL + 16, BL), F32),
            pltpu.VMEM((NZ, 3, 2, CW, LN), BF),
            pltpu.VMEM((NZ, 3, 2, CW, LN), BF),
            pltpu.SemaphoreType.DMA((18,)),
            pltpu.SemaphoreType.DMA((18,)),
        ],
        compiler_params=pltpu.CompilerParams(collective_id=0, has_side_effects=True),
        name="enter",
    )(q, k, v, taps, h, d, w)


def toeplitz(m_buf, channel):
    row = lax.broadcasted_iota(jnp.int32, (LN, LN), 0)
    lane = lax.broadcasted_iota(jnp.int32, (LN, LN), 1)
    keep = lane >= row
    before = jnp.zeros((LN, LN), F32)
    pieces = []
    for piece in range(2 * NZ):
        line = m_buf[pl.ds(piece * CW + channel, 1)]
        turned = pltpu.roll(
            jnp.broadcast_to(line, (LN, LN)), 0, 1, stride=1, stride_axis=0
        )
        pieces.append(jnp.where(keep, turned, before).astype(BF))
        before = turned
    return pieces


def conv_kernel(backward, m_at, x_at, m_ref, x_ref, y_ref, m_buf, x_buf, y_buf):
    n = 2 * NZ
    rows = n * CW
    zero_at, data_at = (rows, 0) if backward else (0, rows)
    for sig in range(2):
        x_buf[sig, pl.ds(zero_at, rows)] = jnp.zeros((rows, LN), F32)
        for src in range(NZ):
            for jj in range(2):
                x_buf[sig, pl.ds(data_at + (2 * src + jj) * CW, CW)] = x_ref[
                    src, x_at + sig, jj
                ].astype(F32)
    for src in range(NZ):
        for jj in range(2):
            m_buf[pl.ds((2 * src + jj) * CW, CW)] = m_ref[src, m_at, jj].astype(F32)

    def one(channel, carry):
        pieces = toeplitz(m_buf, channel)
        lines = []
        for k in range(n):
            first = (k if backward else n - k) * CW + channel
            lines.append(
                jnp.concatenate(
                    [x_buf[sig, pl.ds(first, n, stride=CW)] for sig in range(2)], axis=0
                ).astype(BF)
            )
        left = jnp.concatenate(lines, axis=1)
        if backward:
            y = lax.dot_general(
                left,
                jnp.concatenate(pieces, axis=1),
                (((1,), (1,)), ((), ())),
                preferred_element_type=F32,
            )
        else:
            y = jnp.dot(left, jnp.concatenate(pieces, axis=0), preferred_element_type=F32)
        for sig in range(2):
            y_buf[sig, pl.ds(channel, n, stride=CW)] = y[sig * n : (sig + 1) * n]
        return carry

    lax.fori_loop(0, CW, one, 0)
    for dest in range(NZ):
        for sig in range(2):
            for jj in range(2):
                y_ref[dest, sig, jj] = y_buf[sig, pl.ds((2 * dest + jj) * CW, CW)].astype(BF)


def convolve(backward, m_at, x_at, m, x):
    rows = 2 * NZ * CW
    return pl.pallas_call(
        functools.partial(conv_kernel, backward, m_at, x_at),
        out_shape=jax.ShapeDtypeStruct((NZ, 2, 2, CW, LN), BF),
        in_specs=[VM, VM],
        out_specs=VM,
        scratch_shapes=[
            pltpu.VMEM((rows, LN), F32),
            pltpu.VMEM((2, 2 * rows, LN), F32),
            pltpu.VMEM((2, rows, LN), F32),
        ],
        name="corr" if backward else "conv",
    )(m, x)


def middle_kernel(
    conv_ref, gate_ref, w_ref, wp_ref, target_ref,
    dz_ref,
    conv_buf, own, other, w_own, w_other, goal,
    part_a, part_b, relay, landed, second, relay2, landed2,
    cot_a, cot_b, acc, acc_in, dz_buf, dz_in,
    load_sems, send_sems, recv_sems,
):
    z, c = lax.axis_index("ctx"), lax.axis_index("chan")
    core, chip = lax.rem(c, 2), c // 2
    x, y = chip // NR, lax.rem(chip, NR)
    half = w_ref.shape[1] // 2

    def at(xx, yy):
        return {"chan": (lax.rem(xx, NR) * NR + lax.rem(yy, NR)) * 2 + core}

    partner = {"chan": c + 1 - 2 * core}
    loads = [
        pltpu.make_async_copy(src, dst, load_sems.at[i])
        for i, (src, dst) in enumerate(
            (
                (w_ref.at[:, pl.ds(pl.multiple_of(core * half, LN), half)], w_own),
                (wp_ref, w_other),
                (
                    target_ref.at[
                        :, pl.ds(pl.multiple_of(core * half + chip * BL, LN), BL)
                    ],
                    goal,
                ),
            )
        )
    ]
    for load in loads:
        load.start()
    barrier(
        z_peers(z)
        + [partner]
        + [at(x + o, y) for o in range(1, NR)]
        + [at(x, y + o) for o in range(1, NR)]
    )
    cp = Copies(send_sems, recv_sems)

    def exchange(src, dst):
        arrivals = []
        for off in range(1, NZ):
            to = lax.rem(z + off, NZ)
            arrivals.append(cp.start(src.at[to], dst.at[z], {"ctx": to}))
        dst[z] = src[z]
        for copy in arrivals:
            copy.wait_recv()

    exchange(conv_ref, conv_buf)
    for sig in range(2):
        for jj in range(2):
            turned = conv_buf[:, sig, jj].astype(F32).reshape(BL, LN).T
            own[pl.ds(sig * BL + jj * LN, LN)] = (
                gate_ref[pl.ds(jj * LN, LN)] * turned
            ).astype(BF)
    pair = cp.start(own, other, partner)
    loads[0].wait()
    loads[1].wait()
    pair.wait_recv()

    def product(route, dest):
        part = (part_a, part_b)[route]

        def one(e, carry):
            block = dest * NR + e if route == 0 else e * NR + dest
            columns = pl.ds(pl.multiple_of(block * BL, BL), BL)
            rows = pl.ds(route * BL, BL)
            part[dest, e] = (
                jnp.dot(own[rows], w_own[:, columns], preferred_element_type=F32)
                + jnp.dot(other[rows], w_other[:, columns], preferred_element_type=F32)
            ).astype(BF)
            return carry

        lax.fori_loop(0, NR, one, 0)

    def ahead(along_x, o):
        return at(x + o, y) if along_x else at(x, y + o)

    def place(along_x, o):
        return lax.rem((x if along_x else y) + o, NR)

    def scatter(parts, relays, landings, halves, make):
        axes = [make is not None, make is None]
        kept = []
        for r in range(2):
            if make:
                make(r, place(axes[r], 2))
            far = place(axes[r], 2)
            right, left = ahead(axes[r], 1), ahead(axes[r], 3)
            kept.append(
                [
                    cp.start(halves(parts[r], far, 0), relays.at[r, 0], right),
                    cp.start(halves(parts[r], far, 1), relays.at[r, 1], left),
                ]
            )
        for r in range(2):
            if make:
                make(r, place(axes[r], 1))
            kept[r].append(
                cp.start(
                    halves(parts[r], place(axes[r], 1), 1),
                    landings.at[r, 0, 1],
                    ahead(axes[r], 1),
                )
            )
        for r in range(2):
            if make:
                make(r, place(axes[r], 3))
            kept[r].append(
                cp.start(
                    halves(parts[r], place(axes[r], 3), 0),
                    landings.at[r, 1, 0],
                    ahead(axes[r], 3),
                )
            )
        if make:
            for r in range(2):
                make(r, place(axes[r], 0))
        for side in range(2):
            for r in range(2):
                o = (1, 3)[side]
                kept[r][side].wait_recv()
                chunk = halves(parts[r], place(axes[r], o), side)
                chunk[...] = (chunk[...].astype(F32) + relays[r, side].astype(F32)).astype(BF)
                kept[r].append(cp.start(chunk, landings.at[r, side, side], ahead(axes[r], o)))
        for r in range(2):
            for copy in kept[r][2:]:
                copy.wait_recv()

    def halves_of_blocks(ref, q, h):
        return ref.at[q, pl.ds(2 * h, 2)]

    def halves_of_rows(ref, q, h):
        return ref.at[q, pl.ds(h * LN, LN)]

    parts = (part_a, part_b)
    scatter(parts, relay, landed, halves_of_blocks, product)
    for r in range(2):
        me = (x, y)[r]
        for e in range(NR):
            second[r, e] = (
                parts[r][me, e].astype(F32)
                + landed[r, 0, e // 2, e % 2].astype(F32)
                + landed[r, 1, e // 2, e % 2].astype(F32)
            ).astype(BF)
    scatter((second.at[0], second.at[1]), relay2, landed2, halves_of_rows, None)
    sums = []
    for r in range(2):
        me = (y, x)[r]
        sums.append(
            second[r, me].astype(F32)
            + landed2[r, 0].astype(F32).reshape(BL, BL)
            + landed2[r, 1].astype(F32).reshape(BL, BL)
        )

    loads[2].wait()
    scaling = 1.0 / math.sqrt(NZ * BL)
    bent = jnp.tanh(sums[0] - goal[...].astype(F32))
    cot_a[x, y] = (scaling * bent).astype(BF)
    cot_b[y, x] = (scaling * (1.0 - bent * bent) * sums[1]).astype(BF)

    def gather(stage):
        kept = []
        for r in range(2):
            along_x = (r == 0) == (stage == 1)
            right, left = ahead(along_x, 1), ahead(along_x, 3)
            ref, outer = ((cot_a, x), (cot_b, y))[r]

            def half_at(o, h, ref=ref, outer=outer, along_x=along_x):
                slot = place(along_x, o)
                if stage == 0:
                    return ref.at[outer, slot, pl.ds(h * LN, LN)]
                return ref.at[slot, pl.ds(2 * h, 2)]

            kept.append(
                (
                    half_at,
                    right,
                    left,
                    [
                        cp.start(half_at(0, 0), half_at(0, 0), right),
                        cp.start(half_at(0, 1), half_at(0, 1), left),
                        cp.start(half_at(0, 1), half_at(0, 1), right),
                        cp.start(half_at(0, 0), half_at(0, 0), left),
                    ],
                )
            )
        for half_at, right, left, copies in kept:
            copies[0].wait_recv()
            copies.append(cp.start(half_at(3, 0), half_at(3, 0), right))
            copies[1].wait_recv()
            copies.append(cp.start(half_at(1, 1), half_at(1, 1), left))
        for _, _, _, copies in kept:
            for copy in copies[2:]:
                copy.wait_recv()

    gather(0)
    gather(1)

    nt = (((1,), (1,)), ((), ()))
    acc[...] = jnp.zeros_like(acc)

    def back(q, carry):
        for r, cot in enumerate((cot_a, cot_b)):
            for side, w in enumerate((w_own, w_other)):
                total = None
                for e in range(NR):
                    block = q * NR + e if r == 0 else e * NR + q
                    term = lax.dot_general(
                        cot[q, e],
                        w[:, pl.ds(pl.multiple_of(block * BL, BL), BL)],
                        nt,
                        preferred_element_type=F32,
                    )
                    total = term if total is None else total + term
                acc[side, r] += total
        return carry

    lax.fori_loop(0, NR, back, 0)
    swap = cp.start(acc.at[1], acc_in, partner)
    swap.wait_recv()
    for sig in range(2):
        dz = gate_ref[...] * (acc[0, sig] + acc_in[sig])
        for jj in range(2):
            turned = dz[jj * LN : (jj + 1) * LN].T
            dz_buf[:, sig, jj] = turned.reshape(NZ, CW, LN).astype(BF)
    exchange(dz_buf, dz_in)
    dz_ref[...] = dz_in[...]
    cp.drain()


def middle(conv, gate, w, wp, target):
    half = w.shape[1] // 2
    chunk = (NZ, 2, 2, CW, LN)
    n_copies = 2 * (NZ - 1) + 2 + 4 * 12
    return pl.pallas_call(
        middle_kernel,
        out_shape=jax.ShapeDtypeStruct(chunk, BF),
        in_specs=[VM, VM, ANY, ANY, ANY],
        out_specs=VM,
        scratch_shapes=[
            pltpu.VMEM(chunk, BF),
            pltpu.VMEM((2 * BL, BL), BF),
            pltpu.VMEM((2 * BL, BL), BF),
            pltpu.VMEM((BL, half), BF),
            pltpu.VMEM((BL, half), BF),
            pltpu.VMEM((BL, BL), BF),
            pltpu.VMEM((NR, NR, BL, BL), BF),
            pltpu.VMEM((NR, NR, BL, BL), BF),
            pltpu.VMEM((2, 2, 2, BL, BL), BF),
            pltpu.VMEM((2, 2, 2, 2, BL, BL), BF),
            pltpu.VMEM((2, NR, BL, BL), BF),
            pltpu.VMEM((2, 2, LN, BL), BF),
            pltpu.VMEM((2, 2, 2, LN, BL), BF),
            pltpu.VMEM((NR, NR, BL, BL), BF),
            pltpu.VMEM((NR, NR, BL, BL), BF),
            pltpu.VMEM((2, 2, BL, BL), F32),
            pltpu.VMEM((2, BL, BL), F32),
            pltpu.VMEM(chunk, BF),
            pltpu.VMEM(chunk, BF),
            pltpu.SemaphoreType.DMA((3,)),
            pltpu.SemaphoreType.DMA((n_copies,)),
            pltpu.SemaphoreType.DMA((n_copies,)),
        ],
        compiler_params=pltpu.CompilerParams(collective_id=1, has_side_effects=True),
        name="middle",
    )(conv, gate, w, wp, target)


def leave_kernel(src_ref, a_ref, b_ref, in_buf, send_sems, recv_sems):
    z = lax.axis_index("ctx")
    barrier(z_peers(z))
    cp = Copies(send_sems, recv_sems)
    for off in range(1, NZ):
        to = lax.rem(z + off, NZ)
        cp.start(src_ref.at[to], in_buf.at[z], {"ctx": to})
    in_buf[z] = src_ref[z]
    for copy in cp.made:
        copy.wait_recv()
    for sig, ref in enumerate((a_ref, b_ref)):
        for jj in range(2):
            ref[pl.ds(jj * LN, LN)] = (
                in_buf[:, sig, jj].astype(F32).reshape(BL, LN).T.astype(BF)
            )
    cp.drain()


def leave(src):
    return pl.pallas_call(
        leave_kernel,
        out_shape=(jax.ShapeDtypeStruct((BL, BL), BF),) * 2,
        in_specs=[VM],
        out_specs=(VM, VM),
        scratch_shapes=[
            pltpu.VMEM((NZ, 2, 2, CW, LN), BF),
            pltpu.SemaphoreType.DMA((NZ - 1,)),
            pltpu.SemaphoreType.DMA((NZ - 1,)),
        ],
        compiler_params=pltpu.CompilerParams(collective_id=2, has_side_effects=True),
        name="leave",
    )(src)


def on_device(query_rows, key_rows, value_rows, short_taps, long_filter, direction, w_out, target):
    taps = short_taps.reshape(9, BL)
    gate, got, w_other = enter(
        query_rows, key_rows, value_rows, taps, long_filter, direction, w_out
    )
    conv = convolve(False, 2, 0, got, got)
    dz = middle(conv, gate, w_out, w_other, target)
    grad, hvp = leave(convolve(True, 2, 0, got, dz))
    return grad.astype(F32), hvp.astype(F32)


def solution(mesh):
    in_specs = (
        P("ctx", "chan"),
        P("ctx", "chan"),
        P("ctx", "chan"),
        P(None, None, "chan"),
        P("ctx", "chan"),
        P("ctx", "chan"),
        P("chan", None),
        P("ctx", None),
    )
    out_specs = (P("ctx", "chan"), P("ctx", "chan"))
    return jax.shard_map(
        on_device, mesh=mesh, in_specs=in_specs, out_specs=out_specs, check_vma=False
    )
```

time: 616 us -> 157 us (0.25)
  waiting for transfers between devices: 524 us -> 0 us
  Pallas kernels: 0 us -> 151 us
  matrix products: 41.8 us -> 0 us
  between operations: 14.3 us -> 0.66 us
  starting transfers between devices: 11.8 us -> 0 us
  local copies, waits for them, and re-layouts: 11.1 us -> 1.32 us
    reduce_scatter x2 -> x0, waiting for transfers between devices: 353 us -> none  [the longest x1 210 us: on_device(): lax.psum_scatter(lax.dot_general(w_out, stacked, (((0,), (1,)), ((), ()))...]
    all_gather x4 -> x0, waiting for transfers between devices: 169 us -> none  [the longest x1 65.2 us: on_device(): lax.all_gather(cotangent, 'chan', axis=0, tiled=True)]
    pallas_call x0 -> x5, Pallas kernels: none -> 151 us  [the longest x1 86.7 us: middle(): pl.pallas_call(middle_kernel, out_shape=jax.ShapeDtypeStruct(chunk, BF),...]
    another operation x2 -> x0, matrix products: 27.1 us -> none
    dot_general x2 -> x0, matrix products: 14.8 us -> none  [the longest x1 7.82 us: on_device(): lax.dot_general(w_out, stacked, (((0,), (1,)), ((), ())), preferred_eleme...]
    ppermute x3 -> x0, starting transfers between devices: 11.4 us -> none  [passed_along(): lax.ppermute(value, axis, [(source, source + steps) for source in range(i...]
    slice x8 -> x0, local copies, waits for them, and re-layouts: 6.32 us -> none  [the longest x1 1.79 us: on_device(): return (shares[:, :chan_width], shares[:, chan_width:])]
  transfers between devices with their start and end apart: 9 -> 0, of which waited for: 6 -> 0; matrix products, arithmetic and copies ran while one was open for 1% -> 0% of each run, Pallas kernels for 0% -> 0%
where the time goes in v1:
time: 157 us; the launch traced here: 156 us
  Pallas kernels  151 us (96%)
  other arithmetic  3.25 us (2%)
    pallas_call x1, Pallas kernels, middle(): pl.pallas_call(middle_kernel, out_shape=jax.ShapeDtypeStruct(chunk, BF),...  86.7 us
    pallas_call x2, Pallas kernels, convolve(): pl.pallas_call(functools.partial(conv_kernel, backward, m_at, x_at), out_...  32.1 us
    pallas_call x1, Pallas kernels, enter(): pl.pallas_call(enter_kernel, out_shape=(jax.ShapeDtypeStruct((BL, BL), F3...  19.4 us
    pallas_call x1, Pallas kernels, leave(): pl.pallas_call(leave_kernel, out_shape=(jax.ShapeDtypeStruct((BL, BL), BF...  12.8 us
    convert_element_type x2, other arithmetic, on_device(): return (grad.astype(F32), hvp.astype(F32))  3.25 us

profile of v1, /device:TPU:1, one launch (start us, length us, event | category | flops | bytes accessed | tf_op | source)
XLA Modules:
  0.0 156.2 jit_solution(7665945973131690364)
XLA Ops:
  0.6 1.3 reshape.7.taps_ref
  2.0 19.4 %enter.1 = (f32[256,256]{1,0:T(8,128)}, bf16[8,3,2,32,128]{4,3,2,1,0:T(8,128)(2,1)}, bf16[256,4096]{1,0:T(8,128)(2,1)}) custom-call(bf16[256,256]{1,0:T(8,128)(2,1)} %q_ref.1, bf16[256,256]{1,0:T(8,128)(2,1)} %k_ref.1, bf16[256,256]{1,0:T(8,128)(2,1)} %v_ref.1, f32[9,256]{1,0:T(8,128)} %reshape.7.taps_ref, bf16[256,256]{1,0:T(8,128)(2,1)} %h_ref.1, ...), custom_call_target="tpu_custom_call" | custom-call | tf_op jit(solution)/shard_map/enter/pallas_call | solution.py:116
  21.3 15.7 %conv.1.conv_ref = bf16[8,2,2,32,128]{4,3,2,1,0:T(8,128)(2,1)} custom-call(bf16[8,3,2,32,128]{4,3,2,1,0:T(8,128)(2,1)} %get-tuple-element.7.m_ref.x_ref, bf16[8,3,2,32,128]{4,3,2,1,0:T(8,128)(2,1)} %get-tuple-element.7.m_ref.x_ref), custom_call_target="tpu_custom_call" | custom-call | tf_op jit(solution)/shard_map/conv/pallas_call | solution.py:202
  37.0 86.7 %middle.1.x_ref = bf16[8,2,2,32,128]{4,3,2,1,0:T(8,128)(2,1)} custom-call(bf16[8,2,2,32,128]{4,3,2,1,0:T(8,128)(2,1)} %conv.1.conv_ref, f32[256,256]{1,0:T(8,128)} %get-tuple-element.8.gate_ref, bf16[256,8192]{1,0:T(8,128)(2,1)} %w_ref.3, bf16[256,4096]{1,0:T(8,128)(2,1)} %get-tuple-element.9.wp_ref, bf16[256,8192]{1,0:T(8,128)(2,1)} %target_ref.1), custom_call_target="tpu_custom_call" | custom-call | tf_op jit(solution)/shard_map/middle/pallas_call | solution.py:454
  123.8 16.4 %corr.1.src_ref = bf16[8,2,2,32,128]{4,3,2,1,0:T(8,128)(2,1)} custom-call(bf16[8,3,2,32,128]{4,3,2,1,0:T(8,128)(2,1)} %get-tuple-element.7.m_ref.x_ref, bf16[8,2,2,32,128]{4,3,2,1,0:T(8,128)(2,1)} %middle.1.x_ref), custom_call_target="tpu_custom_call" | custom-call | tf_op jit(solution)/shard_map/corr/pallas_call | solution.py:202
  140.2 12.8 %leave.1 = (bf16[256,256]{1,0:T(8,128)(2,1)}, bf16[256,256]{1,0:T(8,128)(2,1)}) custom-call(bf16[8,2,2,32,128]{4,3,2,1,0:T(8,128)(2,1)} %corr.1.src_ref), custom_call_target="tpu_custom_call" | custom-call | tf_op jit(solution)/shard_map/leave/pallas_call | solution.py:507
  153.0 1.6 %convert_element_type.6 = f32[256,256]{1,0:T(8,128)} convert(bf16[256,256]{1,0:T(8,128)(2,1)} %get-tuple-element.10) | non-fusion elementwise | flops 65536 | bytes 393216 | tf_op jit(solution)/shard_map/convert_element_type | solution.py:530
  154.6 1.6 %convert_element_type.7 = f32[256,256]{1,0:T(8,128)} convert(bf16[256,256]{1,0:T(8,128)(2,1)} %get-tuple-element.11) | non-fusion elementwise | flops 65536 | bytes 393216 | tf_op jit(solution)/shard_map/convert_element_type | solution.py:530

commit v2 on v0

v2 whole, which is shorter than its diff:
```python
import math

import jax
import jax.numpy as jnp
from jax import lax
from jax.experimental import pallas as pl
from jax.experimental.pallas import tpu as pltpu
from jax.sharding import PartitionSpec as P

MESH = pl.DeviceIdType.MESH
BF = jnp.bfloat16
F32 = jnp.float32
VM = pl.BlockSpec(memory_space=pltpu.VMEM)
ANY = pl.BlockSpec(memory_space=pl.ANY)
NZ = 8
NR = 4
BL = 256
LN = 128
NP = 2
CW = BL // NZ
NG = 2
GW = CW // NG
NB = 2 * NZ
N_COPIES = 4 + 2 * 7 + NG * NP * 7 + 2 * NP + NP * 48 + NP * 7 + NG * 7


class Copies:
    def __init__(self, send_sems, recv_sems):
        self.send_sems, self.recv_sems, self.made = send_sems, recv_sems, []

    def start(self, src, dst, device):
        slot = len(self.made)
        copy = pltpu.make_async_remote_copy(
            src_ref=src,
            dst_ref=dst,
            send_sem=self.send_sems.at[slot],
            recv_sem=self.recv_sems.at[slot],
            device_id=device,
            device_id_type=MESH,
        )
        copy.start()
        self.made.append(copy)
        return copy

    def drain(self):
        assert len(self.made) == N_COPIES
        for copy in self.made:
            copy.wait_send()


def arrived(copies):
    for copy in copies:
        copy.wait_recv()


def toeplitz(m_buf, channel):
    row = lax.broadcasted_iota(jnp.int32, (LN, LN), 0)
    lane = lax.broadcasted_iota(jnp.int32, (LN, LN), 1)
    keep = lane >= row
    before = jnp.zeros((LN, LN), F32)
    pieces = []
    for piece in range(NB):
        line = m_buf[pl.ds(piece * CW + channel, 1)]
        turned = pltpu.roll(
            jnp.broadcast_to(line, (LN, LN)), 0, 1, stride=1, stride_axis=0
        )
        pieces.append(jnp.where(keep, turned, before).astype(BF))
        before = turned
    return pieces


def kernel(
    q_ref, k_ref, v_ref, taps_ref, h_ref, d_ref, w_ref, target_ref,
    res_ref,
    halo, ext, gate_t, hdm_out, hdm_in, m_buf, x_buf, y_buf, u_buf,
    conv_out, conv_in, own, other, w_own, w_other, goal,
    part_a, part_b, relay, landed, second, relay2, landed2,
    cot_a, cot_b, acc, acc_in, dz_out, dz_in, res_out, res_in,
    load_sems, send_sems, recv_sems,
):
    z, c = lax.axis_index("ctx"), lax.axis_index("chan")
    core, chip = lax.rem(c, 2), c // 2
    x, y = chip // NR, lax.rem(chip, NR)
    half = w_ref.shape[1] // 2
    cp = Copies(send_sems, recv_sems)

    def at(xx, yy):
        return {"chan": (lax.rem(xx, NR) * NR + lax.rem(yy, NR)) * 2 + core}

    def ahead(along_x, o):
        return at(x + o, y) if along_x else at(x, y + o)

    def place(along_x, o):
        return lax.rem((x if along_x else y) + o, NR)

    partner = {"chan": c + 1 - 2 * core}
    peers = [{"ctx": lax.rem(z + off, NZ)} for off in range(1, NZ)]
    everyone = peers + [partner]
    everyone += [at(x + o, y) for o in (1, 3)] + [at(x, y + o) for o in (1, 3)]
    gate_sem = pltpu.get_barrier_semaphore()
    for device in everyone:
        pl.semaphore_signal(gate_sem, inc=1, device_id=device, device_id_type=MESH)

    loads = [
        pltpu.make_async_copy(src, dst, load_sems.at[i])
        for i, (src, dst) in enumerate(
            (
                (w_ref.at[:, pl.ds(pl.multiple_of(core * half, LN), half)], w_own),
                (
                    target_ref.at[
                        :, pl.ds(pl.multiple_of(core * half + chip * BL, LN), BL)
                    ],
                    goal,
                ),
            )
        )
    ]
    for load in loads:
        load.start()

    def put(value, which):
        for jj in range(2):
            turned = value[jj * LN : (jj + 1) * LN].T
            hdm_out[:, which, jj] = turned.reshape(NZ, CW, LN).astype(BF)

    put(h_ref[...].astype(F32), 0)
    put(d_ref[...].astype(F32), 1)
    pl.semaphore_wait(gate_sem, len(everyone))

    halos = [
        cp.start(ref.at[pl.ds(BL - 16, 16)], halo.at[i], peers[0])
        for i, ref in enumerate((k_ref, v_ref, q_ref))
    ]
    inside = (z > 0).astype(F32)

    def short(i, ref, base):
        halos[i].wait_recv()
        ext[i, pl.ds(0, 16)] = halo[i].astype(F32) * inside
        ext[i, pl.ds(16, BL)] = ref[...].astype(F32)
        return (
            taps_ref[base, pl.ds(0, 1)] * ext[i, pl.ds(16, BL)]
            + taps_ref[base, pl.ds(1, 1)] * ext[i, pl.ds(15, BL)]
            + taps_ref[base, pl.ds(2, 1)] * ext[i, pl.ds(14, BL)]
        )

    def exchange(src_of, dst_of):
        return [
            cp.start(src_of(lax.rem(z + off, NZ)), dst_of(z), peers[off - 1])
            for off in range(1, NZ)
        ]

    put(short(0, k_ref, 1) * short(1, v_ref, 2), 2)
    m_copies = exchange(lambda to: hdm_out.at[to, 2], lambda me: hdm_in.at[me, 2])
    hd_copies = exchange(
        lambda to: hdm_out.at[to, pl.ds(0, 2)], lambda me: hdm_in.at[me, pl.ds(0, 2)]
    )
    w_copy = cp.start(
        w_ref.at[:, pl.ds(pl.multiple_of((1 - core) * half, LN), half)], w_other, partner
    )
    hdm_in[z] = hdm_out[z]
    gate_t[...] = short(2, q_ref, 0).T
    rows = NB * CW
    x_buf[:, pl.ds(0, rows)] = jnp.zeros((2, rows, LN), F32)
    arrived(m_copies)
    for src in range(NZ):
        for jj in range(2):
            m_buf[pl.ds((2 * src + jj) * CW, CW)] = hdm_in[src, 2, jj].astype(F32)

    def build(channel, carry):
        u_buf[channel] = jnp.concatenate(toeplitz(m_buf, channel), axis=1)
        return carry

    lax.fori_loop(0, CW, build, 0)

    def load_x(value_of, first):
        for sig in range(2):
            for src in range(NZ):
                for jj in range(2):
                    x_buf[sig, pl.ds(first + (2 * src + jj) * CW, CW)] = value_of(
                        src, jj, sig
                    ).astype(F32)

    def lines_of(channel, first):
        return jnp.concatenate(
            [
                jnp.concatenate(
                    [x_buf[sig, pl.ds(first(k) + channel, NB, stride=CW)] for sig in range(2)],
                    axis=0,
                ).astype(BF)
                for k in range(NB)
            ],
            axis=1,
        )

    def keep_y(channel, value):
        for sig in range(2):
            y_buf[sig, pl.ds(channel, NB, stride=CW)] = value[sig * NB : (sig + 1) * NB]

    def conv(channel, carry):
        left = lines_of(channel, lambda k: (NB - k) * CW)
        pieces = [u_buf[channel, :, pl.ds(LN * k, LN)] for k in range(NB)]
        keep_y(
            channel,
            jnp.dot(left, jnp.concatenate(pieces, axis=0), preferred_element_type=F32),
        )
        return carry

    def corr(channel, carry):
        left = lines_of(channel, lambda k: k * CW)
        keep_y(
            channel,
            lax.dot_general(
                left, u_buf[channel], (((1,), (1,)), ((), ())), preferred_element_type=F32
            ),
        )
        return carry

    arrived(hd_copies)
    load_x(lambda src, jj, sig: hdm_in[src, sig, jj], rows)
    conv_copies = [[] for _ in range(NP)]
    for g in range(NG):
        lax.fori_loop(g * GW, (g + 1) * GW, conv, 0)
        for jj in range(NP):
            for dest in range(NZ):
                for sig in range(2):
                    conv_out[dest, g, jj, sig] = y_buf[
                        sig, pl.ds((2 * dest + jj) * CW + g * GW, GW)
                    ].astype(BF)
        for jj in range(NP):
            conv_copies[jj] += exchange(
                lambda to, g=g, jj=jj: conv_out.at[to, g, jj],
                lambda me, g=g, jj=jj: conv_in.at[me, g, jj],
            )
    conv_in[z] = conv_out[z]

    pairs = []
    for t in range(NP):
        arrived(conv_copies[t])
        for sig in range(2):
            gated = conv_in[:, :, t, sig].astype(F32).reshape(BL, LN) * gate_t[:, t * LN : (t + 1) * LN]
            own[t, pl.ds(sig * LN, LN)] = gated.T.astype(BF)
        pairs.append(cp.start(own.at[t], other.at[t], partner))
    loads[0].wait()
    w_copy.wait_recv()
    parts = (part_a, part_b)
    crossing = [(part_a, cot_a, True), (part_b, cot_b, False)]

    def product(t, r, dest):
        part = parts[r]
        line = pl.ds(r * LN, LN)

        def one(e, carry):
            block = dest * NR + e if r == 0 else e * NR + dest
            columns = pl.ds(pl.multiple_of(block * BL, BL), BL)
            part[t, dest, e] = (
                jnp.dot(own[t, line], w_own[:, columns], preferred_element_type=F32)
                + jnp.dot(other[t, line], w_other[:, columns], preferred_element_type=F32)
            ).astype(BF)
            return carry

        lax.fori_loop(0, NR, one, 0)

    def products(t, o):
        for r in range(2):
            product(t, r, place(r == 0, o))

    class Scatter:
        def __init__(self, halves, relays, landings, first):
            self.halves, self.relays, self.landings = halves, relays, landings
            self.axes = [first, not first]
            self.far, self.rest = [[], []], [[], []]

        def send_far(self, r):
            a = self.axes[r]
            for side in range(2):
                self.far[r].append(
                    cp.start(
                        self.halves(r, place(a, 2), side),
                        self.relays.at[r, side],
                        ahead(a, (1, 3)[side]),
                    )
                )

        def send_near(self, r, side):
            a, o = self.axes[r], (1, 3)[side]
            self.rest[r].append(
                cp.start(
                    self.halves(r, place(a, o), 1 - side),
                    self.landings.at[r, side, 1 - side],
                    ahead(a, o),
                )
            )

        def pass_on(self):
            for side in range(2):
                for r in range(2):
                    a, o = self.axes[r], (1, 3)[side]
                    self.far[r][side].wait_recv()
                    chunk = self.halves(r, place(a, o), side)
                    chunk[...] = (
                        chunk[...].astype(F32) + self.relays[r, side].astype(F32)
                    ).astype(BF)
                    self.rest[r].append(
                        cp.start(chunk, self.landings.at[r, side, side], ahead(a, o))
                    )

        def wait(self):
            for r in range(2):
                arrived(self.rest[r])

        def start(self):
            for r in range(2):
                self.send_far(r)
            for r in range(2):
                for side in range(2):
                    self.send_near(r, side)

    wide = [
        Scatter(
            lambda r, q, h, t=t: parts[r].at[t, q, pl.ds(2 * h, 2)],
            relay.at[t],
            landed.at[t],
            True,
        )
        for t in range(NP)
    ]
    narrow = [
        Scatter(
            lambda r, q, h, t=t: second.at[t, r, q, pl.ds(h * LN // 2, LN // 2)],
            relay2.at[t],
            landed2.at[t],
            False,
        )
        for t in range(NP)
    ]

    def finish_wide(t):
        wide[t].wait()
        for r in range(2):
            me = (x, y)[r]
            for e in range(NR):
                second[t, r, e] = (
                    parts[r][t, me, e].astype(F32)
                    + landed[t, r, 0, e // 2, e % 2].astype(F32)
                    + landed[t, r, 1, e // 2, e % 2].astype(F32)
                ).astype(BF)
        narrow[t].start()

    class Gather:
        def __init__(self, t, stage):
            self.t, self.stage, self.kept = t, stage, [[], []]

        def half_at(self, r, o, h):
            slot = place((r == 0) == (self.stage == 1), o)
            ref = (cot_a, cot_b)[r]
            if self.stage == 0:
                return ref.at[self.t, (x, y)[r], slot, pl.ds(h * LN, LN)]
            return ref.at[self.t, slot, pl.ds(2 * h, 2)]

        def send(self, r, o, h, side):
            along_x = (r == 0) == (self.stage == 1)
            ref = self.half_at(r, o, h)
            self.kept[r].append(cp.start(ref, ref, ahead(along_x, (1, 3)[side])))

        def start(self):
            for r in range(2):
                self.send(r, 0, 0, 0)
                self.send(r, 0, 1, 1)
            for r in range(2):
                self.send(r, 0, 1, 0)
                self.send(r, 0, 0, 1)

        def pass_on(self):
            for r in range(2):
                self.kept[r][0].wait_recv()
                self.send(r, 3, 0, 0)
                self.kept[r][1].wait_recv()
                self.send(r, 1, 1, 1)

        def wait(self):
            for r in range(2):
                arrived(self.kept[r][2:])

    gathers = [[Gather(t, stage) for stage in range(2)] for t in range(NP)]
    scaling = 1.0 / math.sqrt(NZ * BL)

    def cotangents(t):
        narrow[t].wait()
        sums = [
            second[t, r, (y, x)[r]].astype(F32)
            + landed2[t, r, 0].astype(F32).reshape(LN, BL)
            + landed2[t, r, 1].astype(F32).reshape(LN, BL)
            for r in range(2)
        ]
        bent = jnp.tanh(sums[0] - goal[pl.ds(t * LN, LN)].astype(F32))
        cot_a[t, x, y] = (scaling * bent).T.astype(BF)
        cot_b[t, y, x] = (scaling * (1.0 - bent * bent) * sums[1]).T.astype(BF)
        gathers[t][0].start()

    def widen(t):
        gathers[t][0].wait()
        gathers[t][1].start()

    swaps = [None] * NP

    def back(t):
        gathers[t][1].wait()
        acc[t] = jnp.zeros_like(acc[t])

        def one(q, carry):
            for side, w in enumerate((w_own, w_other)):
                total = None
                for e in range(NR):
                    right = jnp.concatenate([cot_a[t, q, e], cot_b[t, e, q]], axis=1)
                    columns = pl.ds(pl.multiple_of((q * NR + e) * BL, BL), BL)
                    term = jnp.dot(w[:, columns], right, preferred_element_type=F32)
                    total = term if total is None else total + term
                acc[t, side] += total
            return carry

        lax.fori_loop(0, NR, one, 0)
        swaps[t] = cp.start(acc.at[t, 1], acc_in.at[t], partner)

    dz_copies = []

    def send_dz(t):
        swaps[t].wait_recv()
        for sig in range(2):
            lanes = slice(sig * LN, (sig + 1) * LN)
            dz = gate_t[:, t * LN : (t + 1) * LN] * (acc[t, 0, :, lanes] + acc_in[t, :, lanes])
            dz_out[:, t, sig] = dz.reshape(NZ, CW, LN).astype(BF)
        dz_copies.extend(exchange(lambda to: dz_out.at[to, t], lambda me: dz_in.at[me, t]))

    pairs[0].wait_recv()
    products(0, 2)
    for r in range(2):
        wide[0].send_far(r)
    products(0, 1)
    for r in range(2):
        wide[0].send_near(r, 0)
    products(0, 3)
    for r in range(2):
        wide[0].send_near(r, 1)
    products(0, 0)
    pairs[1].wait_recv()
    products(1, 2)
    wide[0].pass_on()
    for r in range(2):
        wide[1].send_far(r)
    products(1, 1)
    products(1, 3)
    for r in range(2):
        for side in range(2):
            wide[1].send_near(r, side)
    products(1, 0)
    finish_wide(0)
    wide[1].pass_on()
    narrow[0].pass_on()
    loads[1].wait()
    cotangents(0)
    finish_wide(1)
    gathers[0][0].pass_on()
    narrow[1].pass_on()
    widen(0)
    cotangents(1)
    gathers[1][0].pass_on()
    gathers[0][1].pass_on()
    widen(1)
    back(0)
    gathers[1][1].pass_on()
    send_dz(0)
    back(1)
    x_buf[:, pl.ds(rows, rows)] = jnp.zeros((2, rows, LN), F32)
    send_dz(1)
    dz_in[z] = dz_out[z]
    arrived(dz_copies)

    load_x(lambda src, jj, sig: dz_in[src, jj, sig], 0)
    res_copies = []
    for g in range(NG):
        lax.fori_loop(g * GW, (g + 1) * GW, corr, 0)
        for dest in range(NZ):
            for jj in range(2):
                for sig in range(2):
                    res_out[dest, g, jj, sig] = y_buf[
                        sig, pl.ds((2 * dest + jj) * CW + g * GW, GW)
                    ].astype(BF)
        res_copies += exchange(
            lambda to, g=g: res_out.at[to, g], lambda me, g=g: res_in.at[me, g]
        )
    res_in[z] = res_out[z]
    arrived(res_copies)
    res_ref[...] = res_in[...]
    cp.drain()


def products_of_a_step(q, k, v, taps, h, d, w, target):
    half = w.shape[1] // 2
    rows = NB * CW
    hdm = (NZ, 3, 2, CW, LN)
    groups = (NZ, NG, NP, 2, GW, LN)
    plain = (NZ, NP, 2, CW, LN)
    return pl.pallas_call(
        kernel,
        out_shape=jax.ShapeDtypeStruct(groups, BF),
        in_specs=[VM] * 6 + [ANY, ANY],
        out_specs=VM,
        scratch_shapes=[
            pltpu.VMEM((3, 16, BL), BF),
            pltpu.VMEM((3, BL + 16, BL), F32),
            pltpu.VMEM((BL, BL), F32),
            pltpu.VMEM(hdm, BF),
            pltpu.VMEM(hdm, BF),
            pltpu.VMEM((rows, LN), F32),
            pltpu.VMEM((2, 2 * rows, LN), F32),
            pltpu.VMEM((2, rows, LN), F32),
            pltpu.VMEM((CW, LN, NB * LN), BF),
            pltpu.VMEM(groups, BF),
            pltpu.VMEM(groups, BF),
            pltpu.VMEM((NP, BL, BL), BF),
            pltpu.VMEM((NP, BL, BL), BF),
            pltpu.VMEM((BL, half), BF),
            pltpu.VMEM((BL, half), BF),
            pltpu.VMEM((BL, BL), BF),
            pltpu.VMEM((NP, NR, NR, LN, BL), BF),
            pltpu.VMEM((NP, NR, NR, LN, BL), BF),
            pltpu.VMEM((NP, 2, 2, 2, LN, BL), BF),
            pltpu.VMEM((NP, 2, 2, 2, 2, LN, BL), BF),
            pltpu.VMEM((NP, 2, NR, LN, BL), BF),
            pltpu.VMEM((NP, 2, 2, LN // 2, BL), BF),
            pltpu.VMEM((NP, 2, 2, 2, LN // 2, BL), BF),
            pltpu.VMEM((NP, NR, NR, BL, LN), BF),
            pltpu.VMEM((NP, NR, NR, BL, LN), BF),
            pltpu.VMEM((NP, 2, BL, BL), F32),
            pltpu.VMEM((NP, BL, BL), F32),
            pltpu.VMEM(plain, BF),
            pltpu.VMEM(plain, BF),
            pltpu.VMEM(groups, BF),
            pltpu.VMEM(groups, BF),
            pltpu.SemaphoreType.DMA((2,)),
            pltpu.SemaphoreType.DMA((N_COPIES,)),
            pltpu.SemaphoreType.DMA((N_COPIES,)),
        ],
        compiler_params=pltpu.CompilerParams(
            collective_id=0, has_side_effects=True, vmem_limit_bytes=60 * 2**20
        ),
        name="step",
    )(q, k, v, taps, h, d, w, target)


def unfold_kernel(src_ref, a_ref, b_ref):
    for sig, ref in enumerate((a_ref, b_ref)):
        for jj in range(2):
            ref[pl.ds(jj * LN, LN)] = src_ref[:, :, jj, sig].astype(F32).reshape(BL, LN).T


def unfold(src):
    return pl.pallas_call(
        unfold_kernel,
        out_shape=(jax.ShapeDtypeStruct((BL, BL), F32),) * 2,
        in_specs=[VM],
        out_specs=(VM, VM),
        name="unfold",
    )(src)


def on_device(*args):
    return unfold(products_of_a_step(*args))


def solution(mesh):
    in_specs = (
        P("ctx", "chan"),
        P("ctx", "chan"),
        P("ctx", "chan"),
        P(None, None, "chan"),
        P("ctx", "chan"),
        P("ctx", "chan"),
        P("chan", None),
        P("ctx", None),
    )
    out_specs = (P("ctx", "chan"), P("ctx", "chan"))
    return jax.shard_map(
        on_device, mesh=mesh, in_specs=in_specs, out_specs=out_specs, check_vma=False
    )
```

time: 616 us -> 136 us (0.22)
  waiting for transfers between devices: 524 us -> 0 us
  Pallas kernels: 0 us -> 135 us
  matrix products: 41.8 us -> 0 us
  between operations: 14.3 us -> 0.64 us
  starting transfers between devices: 11.8 us -> 0 us
  local copies, waits for them, and re-layouts: 11.1 us -> 0 us
  other arithmetic: 9.17 us -> 0 us
    reduce_scatter x2 -> x0, waiting for transfers between devices: 353 us -> none  [the longest x1 210 us: on_device(): lax.psum_scatter(lax.dot_general(w_out, stacked, (((0,), (1,)), ((), ()))...]
    all_gather x4 -> x0, waiting for transfers between devices: 169 us -> none  [the longest x1 65.2 us: on_device(): lax.all_gather(cotangent, 'chan', axis=0, tiled=True)]
    pallas_call x0 -> x2, Pallas kernels: none -> 135 us  [the longest x1 133 us: products_of_a_step(): pl.pallas_call(kernel, out_shape=jax.ShapeDtypeStruct(groups, BF), in_spe...]
    another operation x2 -> x0, matrix products: 27.1 us -> none
    dot_general x2 -> x0, matrix products: 14.8 us -> none  [the longest x1 7.82 us: on_device(): lax.dot_general(w_out, stacked, (((0,), (1,)), ((), ())), preferred_eleme...]
    ppermute x3 -> x0, starting transfers between devices: 11.4 us -> none  [passed_along(): lax.ppermute(value, axis, [(source, source + steps) for source in range(i...]
    convert_element_type x11 -> x0, other arithmetic: 7.03 us -> none  [the longest x3 3.47 us: short_conv(): current.astype(jnp.float32)]
    slice x8 -> x0, local copies, waits for them, and re-layouts: 6.32 us -> none  [the longest x1 1.79 us: on_device(): return (shares[:, :chan_width], shares[:, chan_width:])]
  transfers between devices with their start and end apart: 9 -> 0, of which waited for: 6 -> 0; matrix products, arithmetic and copies ran while one was open for 1% -> 0% of each run, Pallas kernels for 0% -> 0%
where the time goes in v2:
time: 136 us
  Pallas kernels  135 us (99%)
    pallas_call x1, Pallas kernels, products_of_a_step(): pl.pallas_call(kernel, out_shape=jax.ShapeDtypeStruct(groups, BF), in_spe...  133 us

profile of v2, /device:TPU:1, one launch (start us, length us, event | category | flops | bytes accessed | tf_op | source)
XLA Modules:
  0.0 135.9 jit_solution(518003421253147750)
XLA Ops:
  0.6 133.4 %step.1.src_ref = bf16[8,2,2,2,16,128]{5,4,3,2,1,0:T(8,128)(2,1)} custom-call(bf16[256,256]{1,0:T(8,128)(2,1)} %q_ref.1, bf16[256,256]{1,0:T(8,128)(2,1)} %k_ref.1, bf16[256,256]{1,0:T(8,128)(2,1)} %v_ref.1, f32[3,3,256]{2,1,0:T(4,128)} %taps_ref.1, bf16[256,256]{1,0:T(8,128)(2,1)} %h_ref.1, bf16[256,256]{1,0:T(8,128)(2,1)} %d_ref.1, ...), custom_call_target="tpu_custom_call" | custom-call | tf_op jit(solution)/shard_map/step/pallas_call | solution.py:503
  134.1 1.8 %unfold.1 = (f32[256,256]{1,0:T(8,128)}, f32[256,256]{1,0:T(8,128)}) custom-call(bf16[8,2,2,2,16,128]{5,4,3,2,1,0:T(8,128)(2,1)} %step.1.src_ref), custom_call_target="tpu_custom_call" | custom-call | tf_op jit(solution)/shard_map/unfold/pallas_call | solution.py:558

commit v3 on v2

--- a/solution.py
+++ b/solution.py
@@ -21,6 +21,7 @@
 NG = 2
 GW = CW // NG
 NB = 2 * NZ
+BU, CU = 1, 8
 N_COPIES = 4 + 2 * 7 + NG * NP * 7 + 2 * NP + NP * 48 + NP * 7 + NG * 7
 
 
@@ -170,7 +171,7 @@
         u_buf[channel] = jnp.concatenate(toeplitz(m_buf, channel), axis=1)
         return carry
 
-    lax.fori_loop(0, CW, build, 0)
+    lax.fori_loop(0, CW, build, 0, unroll=BU)
 
     def load_x(value_of, first):
         for sig in range(2):
@@ -219,7 +220,7 @@
     load_x(lambda src, jj, sig: hdm_in[src, sig, jj], rows)
     conv_copies = [[] for _ in range(NP)]
     for g in range(NG):
-        lax.fori_loop(g * GW, (g + 1) * GW, conv, 0)
+        lax.fori_loop(g * GW, (g + 1) * GW, conv, 0, unroll=CU)
         for jj in range(NP):
             for dest in range(NZ):
                 for sig in range(2):
@@ -478,7 +479,7 @@
     load_x(lambda src, jj, sig: dz_in[src, jj, sig], 0)
     res_copies = []
     for g in range(NG):
-        lax.fori_loop(g * GW, (g + 1) * GW, corr, 0)
+        lax.fori_loop(g * GW, (g + 1) * GW, corr, 0, unroll=CU)
         for dest in range(NZ):
             for jj in range(2):
                 for sig in range(2):

time: 136 us -> 126 us (0.926)
  Pallas kernels: 135 us -> 126 us
    pallas_call x1, Pallas kernels: 133 us -> 124 us  [products_of_a_step(): pl.pallas_call(kernel, out_shape=jax.ShapeDtypeStruct(groups, BF), in_spe...]
where the time goes in v3:
time: 126 us
  Pallas kernels  126 us (100%)
    pallas_call x1, Pallas kernels, products_of_a_step(): pl.pallas_call(kernel, out_shape=jax.ShapeDtypeStruct(groups, BF), in_spe...  124 us

profile of v3, /device:TPU:1, one launch (start us, length us, event | category | flops | bytes accessed | tf_op | source)
XLA Modules:
  0.0 126.4 jit_solution(12085276547268404665)
XLA Ops:
  0.6 123.9 %step.1.src_ref = bf16[8,2,2,2,16,128]{5,4,3,2,1,0:T(8,128)(2,1)} custom-call(bf16[256,256]{1,0:T(8,128)(2,1)} %q_ref.1, bf16[256,256]{1,0:T(8,128)(2,1)} %k_ref.1, bf16[256,256]{1,0:T(8,128)(2,1)} %v_ref.1, f32[3,3,256]{2,1,0:T(4,128)} %taps_ref.1, bf16[256,256]{1,0:T(8,128)(2,1)} %h_ref.1, bf16[256,256]{1,0:T(8,128)(2,1)} %d_ref.1, ...), custom_call_target="tpu_custom_call" | custom-call | tf_op jit(solution)/shard_map/step/pallas_call | solution.py:504
  124.5 1.8 %unfold.1 = (f32[256,256]{1,0:T(8,128)}, f32[256,256]{1,0:T(8,128)}) custom-call(bf16[8,2,2,2,16,128]{5,4,3,2,1,0:T(8,128)(2,1)} %step.1.src_ref), custom_call_target="tpu_custom_call" | custom-call | tf_op jit(solution)/shard_map/unfold/pallas_call | solution.py:559

commit v4 on v3

--- a/solution.py
+++ b/solution.py
@@ -259,7 +259,7 @@
             ).astype(BF)
             return carry
 
-        lax.fori_loop(0, NR, one, 0)
+        lax.fori_loop(0, NR, one, 0, unroll=True)
 
     def products(t, o):
         for r in range(2):
@@ -419,7 +419,7 @@
                 acc[t, side] += total
             return carry
 
-        lax.fori_loop(0, NR, one, 0)
+        lax.fori_loop(0, NR, one, 0, unroll=True)
         swaps[t] = cp.start(acc.at[t, 1], acc_in.at[t], partner)
 
     dz_copies = []

time: 126 us -> 124 us (0.984)
  Pallas kernels: 126 us -> 124 us
    pallas_call x1, Pallas kernels: 124 us -> 122 us  [products_of_a_step(): pl.pallas_call(kernel, out_shape=jax.ShapeDtypeStruct(groups, BF), in_spe...]
where the time goes in v4:
time: 124 us
  Pallas kernels  124 us (100%)
    pallas_call x1, Pallas kernels, products_of_a_step(): pl.pallas_call(kernel, out_shape=jax.ShapeDtypeStruct(groups, BF), in_spe...  122 us

profile of v4, /device:TPU:1, one launch (start us, length us, event | category | flops | bytes accessed | tf_op | source)
XLA Modules:
  0.0 124.3 jit_solution(17475137797375873370)
XLA Ops:
  0.6 121.8 %step.1.src_ref = bf16[8,2,2,2,16,128]{5,4,3,2,1,0:T(8,128)(2,1)} custom-call(bf16[256,256]{1,0:T(8,128)(2,1)} %q_ref.1, bf16[256,256]{1,0:T(8,128)(2,1)} %k_ref.1, bf16[256,256]{1,0:T(8,128)(2,1)} %v_ref.1, f32[3,3,256]{2,1,0:T(4,128)} %taps_ref.1, bf16[256,256]{1,0:T(8,128)(2,1)} %h_ref.1, bf16[256,256]{1,0:T(8,128)(2,1)} %d_ref.1, ...), custom_call_target="tpu_custom_call" | custom-call | tf_op jit(solution)/shard_map/step/pallas_call | solution.py:504
  122.4 1.8 %unfold.1 = (f32[256,256]{1,0:T(8,128)}, f32[256,256]{1,0:T(8,128)}) custom-call(bf16[8,2,2,2,16,128]{5,4,3,2,1,0:T(8,128)(2,1)} %step.1.src_ref), custom_call_target="tpu_custom_call" | custom-call | tf_op jit(solution)/shard_map/unfold/pallas_call | solution.py:559
